TPU v7x, 32 devices: a whole 2x2x4 slice. The times are simulated.
32 devices in a mesh: seq: 8 (over y, x, core), head: 4 (over z).
Axes of the slice: x: 2, y: 2, z: 4, core: 2. Of those that a mesh axis runs over, the one named last changes fastest.
Arguments:
- queries: bfloat16 [4096, 2048], P('seq', 'head'), may hold values from -6 to 6
- key_rows: bfloat16 [4096, 2048], P('seq', 'head'), may hold values from -6 to 6
- values: bfloat16 [4096, 2048], P('seq', 'head'), may hold values from -6 to 6
- write_rate: float32 [16, 4096], P('head', 'seq'), may hold values from 0.001 to 0.95
- decay_rate: float32 [16, 4096], P('head', 'seq'), may hold values from 0 to 1.5
- level_weight: int32 [64, 7], P('seq'), may hold values from 1 to 64
- out_weight: bfloat16 [2048, 2048], P('head'), may hold values from -0.125 to 0.125
Outputs:
- mixed_out: bfloat16 [4096, 2048], P(('seq', 'head'))
All inputs are finite; a program needn't handle non-finite values.
Results may differ from a plain program's by a relative error of at most 0.0049.
Values sent between devices are 32-bit elements; how exact they have to be, the bound alone decides.
A program may use at most 128 MiB of HBM per device.

v0:
```python
import functools

import jax
import jax.numpy as jnp
from jax import lax
from jax.experimental import pallas as pl
from jax.experimental.pallas import tpu as pltpu
from jax.sharding import PartitionSpec as P

BLOCK = 64
NORM_EPS = 1e-06
LEVEL_UNIT = 0.125
F32 = jnp.float32
BF16 = jnp.bfloat16
NN = (((1,), (0,)), ((), ()))
NT = (((1,), (1,)), ((), ()))
TN = (((0,), (0,)), ((), ()))


def dot(left, right, dims=NN):
    return lax.dot_general(left, right, dims, preferred_element_type=F32)


def exact_dot(left, right, dims=NN):
    return lax.dot_general(
        left, right, dims, precision=lax.Precision.HIGHEST, preferred_element_type=F32
    )


def split(x):
    high = x.astype(BF16)
    return high, (x - high.astype(F32)).astype(BF16)


def dot3(left, right):
    (lh, ll), (rh, rl) = left, right
    return dot(lh, rh) + (dot(lh, rl) + dot(ll, rh))


def local_kernel(q_ref, k_ref, v_ref, beta_ref, decay_ref, lw_ref, g_ref, o_ref, ab_ref):
    blocks = q_ref.shape[0] // BLOCK
    size = q_ref.shape[1]
    every = range(blocks)
    row_at = lax.broadcasted_iota(jnp.int32, (BLOCK, BLOCK), 0)
    col_at = lax.broadcasted_iota(jnp.int32, (BLOCK, BLOCK), 1)
    causal, strictly, diag = row_at >= col_at, row_at > col_at, row_at == col_at
    lower = jnp.where(causal, 1.0, 0.0).astype(F32)
    eye = jnp.where(diag, 1.0, 0.0).astype(F32)
    beta_rows = beta_ref[0]
    decay_rows = decay_ref[0]
    log_rows = -exact_dot(decay_rows, lower, NT)
    log_cols = -exact_dot(lower, decay_rows, NT)
    beta_cols = exact_dot(eye, beta_rows, NT)

    q = [q_ref[c * BLOCK : (c + 1) * BLOCK, :] for c in every]
    k = [k_ref[c * BLOCK : (c + 1) * BLOCK, :] for c in every]
    v = [v_ref[c * BLOCK : (c + 1) * BLOCK, :] for c in every]
    power, inverse, scores, pre = [], [], [], []
    for c in every:
        log_row, log_col = log_rows[c : c + 1, :], log_cols[:, c : c + 1]
        gram = dot(k[c], k[c], NT)
        on_diag = jnp.where(diag, gram, 0.0)
        rk_row = lax.rsqrt(jnp.sum(on_diag, axis=0, keepdims=True) + NORM_EPS)
        rk_col = lax.rsqrt(jnp.sum(on_diag, axis=1, keepdims=True) + NORM_EPS)
        qf = q[c].astype(F32)
        rq_col = lax.rsqrt(jnp.sum(qf * qf, axis=1, keepdims=True) + NORM_EPS)
        ratios = jnp.where(causal, jnp.exp(jnp.where(causal, log_col - log_row, 0.0)), 0.0)
        scaled = ratios * rk_row
        n = jnp.where(strictly, (beta_cols[:, c : c + 1] * rk_col) * (scaled * gram), 0.0)
        power.append(n)
        inverse.append(eye - n)
        scores.append(dot(q[c], k[c], NT) * (scaled * rq_col))
        end = log_row[:, BLOCK - 1 :]
        pre.append((
            beta_rows[c : c + 1, :] * rk_row * jnp.exp(log_row),
            beta_rows[c : c + 1, :],
            rk_col * jnp.exp(end - log_col),
            jnp.exp(log_col) * rq_col * qf,
            jnp.exp(end),
        ))
    steps = (BLOCK - 1).bit_length() - 1
    for c in every:
        ph, plo = split(power[c])
        power[c] = dot3((ph, plo), (ph, plo))
    for step in range(steps):
        for c in every:
            ph, plo = split(power[c])
            ih, ilo = split(inverse[c])
            if step < steps - 1:
                out = dot3(
                    (jnp.concatenate([ph, ih], 0), jnp.concatenate([plo, ilo], 0)), (ph, plo)
                )
                power[c] = out[:BLOCK]
                inverse[c] = inverse[c] + out[BLOCK:]
            else:
                inverse[c] = inverse[c] + dot3((ih, ilo), (ph, plo))
    maps, fronts, inside = [], [], []
    eye_state = jnp.where(
        lax.broadcasted_iota(jnp.int32, (size, size), 0)
        == lax.broadcasted_iota(jnp.int32, (size, size), 1),
        1.0,
        0.0,
    ).astype(F32)
    for c in every:
        key_scale, value_scale, tail_scale, q_part, gamma_end = pre[c]
        kh, kl = split(inverse[c] * key_scale)
        vh, vl = split(inverse[c] * value_scale)
        w = jnp.concatenate([dot(kh, k[c]) + dot(kl, k[c]), dot(vh, v[c]) + dot(vl, v[c])], 1)
        th, tl = split(w * tail_scale)
        carry = dot(k[c], th, TN) + dot(k[c], tl, TN)
        maps.append(
            jnp.concatenate([gamma_end * eye_state - carry[:, :size], carry[:, size:]], 1)
        )
        reads = dot3(split(scores[c]), split(w))
        fronts.append(q_part - reads[:, :size])
        inside.append(reads[:, size:])
    levels = [maps]
    while len(maps) > 1:
        merged = []
        for left, right in zip(maps[0::2], maps[1::2]):
            out = dot3(split(right[:, :size]), split(left))
            merged.append(
                jnp.concatenate([out[:, :size], out[:, size:] + right[:, size:]], 1)
            )
        maps = merged
        levels.append(maps)
    ab_ref[0] = levels[-1][0]
    splits = [[split(m) for m in level] for level in levels[:-1]]
    for c in every:
        front = fronts[c]
        total = lw_ref[c, 0].astype(F32) * LEVEL_UNIT * inside[c]
        for bit in range(len(splits)):
            if c >> bit & 1:
                out = dot3(split(front), splits[bit][(c >> bit) - 1])
                total = total + lw_ref[c, 1 + bit].astype(F32) * LEVEL_UNIT * out[:, size:]
                front = out[:, :size]
        g_ref[c * BLOCK : (c + 1) * BLOCK, :] = front
        o_ref[c * BLOCK : (c + 1) * BLOCK, :] = total


def local_part(queries, key_rows, values, write_rate, decay_rate, level_weight):
    heads = write_rate.shape[0]
    tokens = queries.shape[0]
    size = queries.shape[1] // heads
    blocks = tokens // BLOCK
    wide = pl.BlockSpec((tokens, size), lambda h: (0, h))
    rates = pl.BlockSpec((1, blocks, BLOCK), lambda h: (h, 0, 0))
    return pl.pallas_call(
        local_kernel,
        grid=(heads,),
        in_specs=[wide, wide, wide, rates, rates, pl.BlockSpec(memory_space=pltpu.SMEM)],
        out_specs=[wide, wide, pl.BlockSpec((1, size, 2 * size), lambda h: (h, 0, 0))],
        out_shape=[
            jax.ShapeDtypeStruct((tokens, heads * size), F32),
            jax.ShapeDtypeStruct((tokens, heads * size), F32),
            jax.ShapeDtypeStruct((heads, size, 2 * size), F32),
        ],
        name="local_part",
    )(
        queries,
        key_rows,
        values,
        write_rate.reshape(heads, blocks, BLOCK),
        decay_rate.reshape(heads, blocks, BLOCK),
        level_weight,
    )


def per_device(queries, key_rows, values, write_rate, decay_rate, level_weight, out_weight):
    heads = write_rate.shape[0]
    tokens = queries.shape[0]
    size = queries.shape[1] // heads
    blocks = tokens // BLOCK
    depth = blocks.bit_length() - 1
    front, total, pair = local_part(
        queries, key_rows, values, write_rate, decay_rate, level_weight
    )
    mm = functools.partial(jnp.matmul, precision=lax.Precision.HIGHEST)
    spans = lax.all_gather(pair[None], "seq", axis=0, tiled=True)
    place = lax.axis_index("seq")
    bits = lax.axis_size("seq").bit_length() - 1
    levels = [spans]
    for _ in range(bits - 1):
        left, right = spans[0::2], spans[1::2]
        out = mm(right[..., :size], left)
        spans = out.at[..., size:].add(right[..., size:])
        levels.append(spans)
    weights = jnp.repeat(level_weight.astype(F32) * LEVEL_UNIT, BLOCK, axis=0)
    front = jnp.moveaxis(front.reshape(tokens, heads, size), 1, 0)
    added = jnp.zeros_like(front)
    for bit in range(bits):
        pick = jnp.maximum(jnp.right_shift(place, bit) - 1, 0)
        span = lax.dynamic_index_in_dim(levels[bit], pick, 0, keepdims=False)
        is_set = jnp.bitwise_and(jnp.right_shift(place, bit), 1) == 1
        out = mm(front, span)
        added = added + jnp.where(
            is_set, weights[:, 1 + depth + bit][None, :, None] * out[..., size:], 0.0
        )
        front = jnp.where(is_set, out[..., :size], front)
    heads_out = (total + jnp.moveaxis(added, 0, 1).reshape(tokens, heads * size)).astype(BF16)
    mixed_out = lax.psum_scatter(
        jnp.dot(heads_out, out_weight, preferred_element_type=F32),
        "head",
        scatter_dimension=0,
        tiled=True,
    )
    return mixed_out.astype(BF16)


def solution(mesh):
    placed = (
        P("seq", "head"),
        P("seq", "head"),
        P("seq", "head"),
        P("head", "seq"),
        P("head", "seq"),
        P("seq", None),
        P("head", None),
    )
    return jax.shard_map(
        per_device, mesh=mesh, in_specs=placed, out_specs=P(("seq", "head"), None), check_vma=False
    )
```

profile of v0, /device:TPU:15, one launch (start us, length us, event | category | flops | bytes accessed | tf_op | source)
XLA Modules:
  0.0 173.5 jit_solution(3392662334791692528)
XLA Ops:
  6.5 0.0 copy-start
  6.5 0.0 all-gather.3.cloned.1.call-start
  6.5 1.5 reshape.87.beta_ref
  8.1 1.4 reshape.88.decay_ref
  9.4 0.0 copy-start.2
  9.4 21.9 %local_part.1 = (f32[512,512]{1,0:T(8,128)}, f32[512,512]{1,0:T(8,128)}, f32[4,128,256]{2,1,0:T(8,128)}) custom-call(bf16[512,512]{1,0:T(8,128)(2,1)} %q_ref.1, bf16[512,512]{1,0:T(8,128)(2,1)} %k_ref.1, bf16[512,512]{1,0:T(8,128)(2,1)} %v_ref.1, f32[4,8,64]{2,1,0:T(8,128)} %reshape.87.beta_ref, f32[4,8,64]{2,1,0:T(8,128)} %reshape.88.decay_ref, s32[8,7]{1,0:T(8,128)} %lw_ref.1), custom_call_target="tpu_custom_call" | custom-call | tf_op jit(solution)/shard_map/local_part/pallas_call | solution.py:148
  31.3 0.0 all-gather.3.cloned.1.call-update
  31.3 0.2 reduce-scatter.2.cloned.1.call-start
  31.6 1.6 copy.37
  33.1 0.0 copy-done.2
  33.1 0.1 copy.23
  33.2 0.1 broadcast_in_dim.12
  33.3 0.1 reshape.89
  33.4 35.2 %all-gather.3.cloned.1.call-done = f32[32,128,256]{2,1,0:T(8,128)} async-done(((f32[4,128,256]{2,1,0:T(8,128)}), f32[32,128,256]{2,1,0:T(8,128)}) %all-gather.3.cloned.1.call-update) | async-done | bytes 4194320 | tf_op jit(solution)/shard_map/all_gather | solution.py:179
  68.6 0.0 copy-start.1
  68.6 1.9 %slice.110 = f32[4,4,128,256]{3,2,1,0:T(8,128)S(1)} slice(f32[8,4,128,256]{3,2,1,0:T(8,128)} %bitcast.26), slice={[1:8:2], [0:4:1], [0:128:1], [0:256:1]} | slice | bytes 4194304 | tf_op jit(solution)/shard_map/slice | solution.py:184
  70.5 0.9 copy-done.1
  71.5 1.9 %fusion = f32[4,4,128,256]{3,2,1,0:T(8,128)S(1)} fusion(f32[8,4,128,256]{3,2,1,0:T(8,128)S(1)} %bitcast.27, f32[4,4,128,256]{3,2,1,0:T(8,128)S(1)} %slice.110), kind=kOutput, calls=%fused_computation | convolution fusion | flops 805306368 | bytes 5242880 | tf_op jit(solution)/shard_map/dot_general | solution.py:185
  73.4 0.3 fusion.6
  73.6 0.1 slice.118
  73.7 1.0 fusion.9
  74.8 0.1 fusion.12
  74.9 1.9 %fusion.14 = f32[4,512,256]{1,2,0:T(8,128)S(1)} fusion(f32[4,512,128]{1,2,0:T(8,128)S(1)} %bitcast.23, f32[8,4,128,256]{3,2,1,0:T(8,128)S(1)} %bitcast.28, s32[]{:T(128)S(6)} %max.9), kind=kOutput, calls=%fused_computation.22 | convolution fusion | flops 805306368 | bytes 3670020 | tf_op jit(solution)/shard_map/dot_general | solution.py:195
  76.8 1.9 %fusion.16 = f32[4,512,256]{1,2,0:T(8,128)S(1)} fusion(f32[4,4,128,256]{3,2,1,0:T(8,128)S(1)} %fusion.6, s32[]{:T(128)S(6)} %max.10, f32[4,512,128]{1,2,0:T(8,128)S(1)} %bitcast.24, f32[4,512,256]{1,2,0:T(8,128)S(1)} %fusion.14, pred[]{:T(512)S(6)} %eq.9), kind=kOutput, calls=%fused_computation.24 | convolution fusion | flops 805568512 | bytes 4718597 | tf_op jit(solution)/shard_map/dot_general | solution.py:195
  78.7 2.4 %fusion.3 = f32[4,512,128]{1,2,0:T(8,128)} fusion(f32[4,512,256]{1,2,0:T(8,128)S(1)} %fusion.16, f32[4,512,256]{1,2,0:T(8,128)S(1)} %fusion.14, f32[512]{0:T(512)S(1)} %bitcast.31, f32[512]{0:T(512)S(1)} %bitcast.32, f32[512]{0:T(512)S(1)} %bitcast.30, pred[]{:T(512)S(6)} %eq.11, pred[]{:T(512)S(6)} %eq.10, pred[]{:T(512)S(6)} %eq.9, ...), kind=kOutput, calls=%fused_computation.4 | convolution fusion | flops 405274624 | bytes 6562304 | tf_op jit(solution)/shard_map/dot_general | solution.py:195
  81.1 1.6 copy.38
  82.7 0.0 copy-done
  82.7 4.4 %fusion.11 = f32[512,2048]{1,0:T(8,128)} fusion(bf16[512,2048]{1,0:T(8,128)(2,1)S(1)} %copy-done, f32[512,512]{1,0:T(8,128)} %get-tuple-element.32, f32[512,512]{1,0:T(8,128)S(1)} %copy.38), kind=kOutput, calls=%fused_computation.18 | convolution fusion | flops 1074266112 | bytes 8388608 | tf_op jit(solution)/shard_map/dot_general | solution.py:202
  87.1 0.0 reduce-scatter.2.cloned.1.call-update
  87.1 77.4 %reduce-scatter.2.cloned.1.call-done = f32[128,2048]{1,0:T(8,128)} async-done(((f32[512,2048]{1,0:T(8,128)}), f32[128,2048]{1,0:T(8,128)}) %reduce-scatter.2.cloned.1.call-update) | async-done | bytes 1048592 | tf_op jit(solution)/shard_map/reduce_scatter | solution.py:201
  164.5 2.1 %convert_element_type.11 = bf16[128,2048]{1,0:T(8,128)(2,1)} convert(f32[128,2048]{1,0:T(8,128)} %reduce-scatter.2.cloned.1.call-done) | non-fusion elementwise | flops 262144 | bytes 1572864 | tf_op jit(solution)/shard_map/convert_element_type | solution.py:207
  (3 shorter events, 0.1 us)
Async XLA Ops:
  6.5 76.1 %copy-start = (bf16[512,2048]{1,0:T(8,128)(2,1)S(1)}, bf16[512,2048]{1,0:T(8,128)(2,1)}, u32[]{:S(2)}) copy-start(bf16[512,2048]{1,0:T(8,128)(2,1)} %param.17) | copy-start | bytes 6291460
  6.5 62.1 %all-gather.3.cloned.1.call-start = ((), (), s32[]{:S(2)}) async-start(), calls=%async_computation.2 | async-start | bytes 4718592 | tf_op jit(solution)/shard_map/all_gather | solution.py:179
  9.4 23.7 %copy-start.2 = (s32[8,7]{1,0:T(8,128)S(1)}, s32[8,7]{1,0:T(8,128)}, u32[]{:S(2)}) copy-start(s32[8,7]{1,0:T(8,128)} %lw_ref.1) | copy-start | bytes 676
  31.3 133.2 %reduce-scatter.2.cloned.1.call-start = ((), (), s32[]{:S(2)}) async-start(), calls=%async_computation.1 | async-start | bytes 5242880 | tf_op jit(solution)/shard_map/reduce_scatter | solution.py:201
  68.6 2.8 %copy-start.1 = (f32[32,128,256]{2,1,0:T(8,128)S(1)}, f32[32,128,256]{2,1,0:T(8,128)}, u32[]{:S(2)}) copy-start(f32[32,128,256]{2,1,0:T(8,128)} %all-gather.3.cloned.1.call-done) | copy-start | bytes 12582916
Sparse Core Ops, SparseCore 0:
  31.4 37.1 all-gather.2
  87.3 77.2 reduce-scatter.1
where the time goes:
time: 175 us; the launch traced here: 173 us
  waiting for transfers between devices  113 us (65%)
  Pallas kernels  21.9 us (13%)
  matrix products  13.5 us (8%)
  between operations  13.5 us (8%)
  local copies, waits for them, and re-layouts  9.17 us (5%)
  other arithmetic  2.48 us (1%)
    reduce_scatter x1, waiting for transfers between devices, per_device(): lax.psum_scatter(jnp.dot(heads_out, out_weight, preferred_element_type=F3...  77.4 us
    all_gather x1, waiting for transfers between devices, per_device(): spans = lax.all_gather(pair[None], 'seq', axis=0, tiled=True)  35.2 us
    pallas_call x1, Pallas kernels, local_part(): pl.pallas_call(local_kernel, grid=(heads,), in_specs=[wide, wide, wide, r...  21.9 us
    dot_general x3, matrix products, per_device(): out = mm(front, span)  6.16 us
    dot_general x1, matrix products, per_device(): jnp.dot(heads_out, out_weight, preferred_element_type=F32)  4.43 us
  transfers between devices with their start and end apart: 2, of which 2 were waited for; matrix products, arithmetic and copies ran while one was open for 1% of the time, Pallas kernels for 0%

commit v1 on v0

--- a/solution.py
+++ b/solution.py
@@ -1,5 +1,3 @@
-import functools
-
 import jax
 import jax.numpy as jnp
 from jax import lax
@@ -12,6 +10,7 @@
 LEVEL_UNIT = 0.125
 F32 = jnp.float32
 BF16 = jnp.bfloat16
+MESH = pl.DeviceIdType.MESH
 NN = (((1,), (0,)), ((), ()))
 NT = (((1,), (1,)), ((), ()))
 TN = (((0,), (0,)), ((), ()))
@@ -37,7 +36,7 @@
     return dot(lh, rh) + (dot(lh, rl) + dot(ll, rh))
 
 
-def local_kernel(q_ref, k_ref, v_ref, beta_ref, decay_ref, lw_ref, g_ref, o_ref, ab_ref):
+def local_kernel(q_ref, k_ref, v_ref, beta_ref, decay_ref, lw_ref, g_ref, o_ref, a_ref, b_ref):
     blocks = q_ref.shape[0] // BLOCK
     size = q_ref.shape[1]
     every = range(blocks)
@@ -124,7 +123,8 @@
             )
         maps = merged
         levels.append(maps)
-    ab_ref[0] = levels[-1][0]
+    a_ref[0] = levels[-1][0][:, :size]
+    b_ref[0] = levels[-1][0][:, size:]
     splits = [[split(m) for m in level] for level in levels[:-1]]
     for c in every:
         front = fronts[c]
@@ -144,16 +144,18 @@
     size = queries.shape[1] // heads
     blocks = tokens // BLOCK
     wide = pl.BlockSpec((tokens, size), lambda h: (0, h))
+    state = pl.BlockSpec((1, size, size), lambda h: (h, 0, 0))
     rates = pl.BlockSpec((1, blocks, BLOCK), lambda h: (h, 0, 0))
     return pl.pallas_call(
         local_kernel,
         grid=(heads,),
         in_specs=[wide, wide, wide, rates, rates, pl.BlockSpec(memory_space=pltpu.SMEM)],
-        out_specs=[wide, wide, pl.BlockSpec((1, size, 2 * size), lambda h: (h, 0, 0))],
+        out_specs=[wide, wide, state, state],
         out_shape=[
             jax.ShapeDtypeStruct((tokens, heads * size), F32),
             jax.ShapeDtypeStruct((tokens, heads * size), F32),
-            jax.ShapeDtypeStruct((heads, size, 2 * size), F32),
+            jax.ShapeDtypeStruct((heads, size, size), F32),
+            jax.ShapeDtypeStruct((heads, size, size), F32),
         ],
         name="local_part",
     )(
@@ -166,45 +168,225 @@
     )
 
 
-def per_device(queries, key_rows, values, write_rate, decay_rate, level_weight, out_weight):
-    heads = write_rate.shape[0]
-    tokens = queries.shape[0]
-    size = queries.shape[1] // heads
+def merge_kernel(
+    g_ref, o_ref, a_ref, b_ref, lw_ref, w_ref, out_ref,
+    front, total, span_a, span_b, got_a, got_b, part, got,
+    span_send, span_recv, part_send, part_recv,
+):
+    runs, groups = lax.axis_size("seq"), lax.axis_size("head")
+    place, rank = lax.axis_index("seq"), lax.axis_index("head")
+    bits = runs.bit_length() - 1
+    heads, size = a_ref.shape[0], a_ref.shape[1]
+    tokens = g_ref.shape[0]
     blocks = tokens // BLOCK
     depth = blocks.bit_length() - 1
-    front, total, pair = local_part(
+    rows = tokens // groups
+    pieces = got.shape[2]
+    width = w_ref.shape[1] // pieces
+
+    barrier = pltpu.get_barrier_semaphore()
+    for hop in range(1, runs):
+        pl.semaphore_signal(
+            barrier, inc=1, device_id={"seq": lax.rem(place + hop, runs)}, device_id_type=MESH
+        )
+    has_below, has_above = rank > 0, rank < groups - 1
+
+    @pl.when(has_below)
+    def _():
+        pl.semaphore_signal(barrier, inc=1, device_id={"head": rank - 1}, device_id_type=MESH)
+
+    @pl.when(has_above)
+    def _():
+        pl.semaphore_signal(barrier, inc=1, device_id={"head": rank + 1}, device_id_type=MESH)
+
+    pl.semaphore_wait(
+        barrier, runs - 1 + has_below.astype(jnp.int32) + has_above.astype(jnp.int32)
+    )
+
+    def span_copy(level, fan, what):
+        source = ((b_ref, span_b), (a_ref, span_a))[what]
+        return pltpu.make_async_remote_copy(
+            src_ref=source[0] if level == 0 else source[1].at[level - 1],
+            dst_ref=(got_b, got_a)[what].at[level],
+            send_sem=span_send.at[what, level, fan],
+            recv_sem=span_recv.at[what, level],
+            device_id={"seq": lax.rem(place + 1 + fan, runs)},
+            device_id_type=MESH,
+        )
+
+    def own(level):
+        if level == 0:
+            return a_ref, b_ref
+        return span_a.at[level - 1], span_b.at[level - 1]
+
+    total[...] = o_ref[...]
+    front[...] = g_ref[...]
+    for level in range(bits):
+        low = 2**level
+        inner = place & (2 * low - 1)
+        later = (place >> (level + 1)) > 0
+        is_source = inner == low - 1
+        bit_set = inner >= low
+
+        @pl.when(is_source)
+        def _():
+            for fan in range(low):
+                span_copy(level, fan, 0).start()
+
+            @pl.when(later)
+            def _():
+                for fan in range(low):
+                    span_copy(level, fan, 1).start()
+
+        @pl.when(bit_set)
+        def _():
+            span_copy(level, 0, 0).wait_recv()
+
+            @pl.when(later)
+            def _():
+                span_copy(level, 0, 1).wait_recv()
+
+            if level < bits - 1:
+
+                @pl.when(inner == 2 * low - 1)
+                def _():
+                    own_a, own_b = own(level)
+
+                    @pl.loop(0, heads)
+                    def _(h):
+                        turn = split(own_a[h])
+                        span_b[level, h] = dot3(turn, split(got_b[level, h])) + own_b[h]
+
+                        @pl.when(later)
+                        def _():
+                            span_a[level, h] = dot3(turn, split(got_a[level, h]))
+
+    for level in range(bits):
+        low = 2**level
+        inner = place & (2 * low - 1)
+        later = (place >> (level + 1)) > 0
+
+        @pl.when(inner >= low)
+        def _():
+            @pl.loop(0, heads)
+            def _(h):
+                columns = pl.ds(pl.multiple_of(h * size, size), size)
+                now = split(front[:, columns])
+                add = dot3(now, split(got_b[level, h]))
+                for c in range(blocks):
+                    at = slice(c * BLOCK, (c + 1) * BLOCK)
+                    scale = lw_ref[c, 1 + depth + level].astype(F32) * LEVEL_UNIT
+                    total[at, columns] = total[at, columns] + scale * add[at]
+
+                @pl.when(later)
+                def _():
+                    front[:, columns] = dot3(now, split(got_a[level, h]))
+
+        @pl.when(inner == low - 1)
+        def _():
+            for fan in range(low):
+                span_copy(level, fan, 0).wait_send()
+
+            @pl.when(later)
+            def _():
+                for fan in range(low):
+                    span_copy(level, fan, 1).wait_send()
+
+    for chunk in sorted(range(groups), key=lambda d: min(d, groups - 1 - d)):
+        heads_out = total[chunk * rows : (chunk + 1) * rows, :].astype(BF16)
+        for piece in range(pieces):
+            part[chunk, piece] = dot(heads_out, w_ref[:, piece * width : (piece + 1) * width])
+
+    def part_copy(way, chunk, piece):
+        return pltpu.make_async_remote_copy(
+            src_ref=part.at[chunk, piece],
+            dst_ref=got.at[way, chunk, piece],
+            send_sem=part_send.at[chunk, piece],
+            recv_sem=part_recv.at[way, chunk, piece],
+            device_id={"head": rank + 1 if way == 0 else rank - 1},
+            device_id_type=MESH,
+        )
+
+    def pass_on(way, chunk):
+        for piece in range(pieces):
+
+            @pl.when((has_below, has_above)[way])
+            def _():
+                part_copy(way, chunk, piece).wait_recv()
+                part[chunk, piece] = part[chunk, piece] + got[way, chunk, piece]
+
+            part_copy(way, chunk, piece).start()
+
+    for step in range(groups - 1):
+        up, down = groups - 1 - step, step
+
+        @pl.when(rank < up)
+        def _():
+            pass_on(0, up)
+
+        @pl.when(rank > down)
+        def _():
+            pass_on(1, down)
+
+    for chunk in range(groups):
+
+        @pl.when(rank == chunk)
+        def _():
+            for piece in range(pieces):
+                mixed = part[chunk, piece]
+                if chunk > 0:
+                    part_copy(0, chunk, piece).wait_recv()
+                    mixed = mixed + got[0, chunk, piece]
+                if chunk < groups - 1:
+                    part_copy(1, chunk, piece).wait_recv()
+                    mixed = mixed + got[1, chunk, piece]
+                out_ref[:, piece * width : (piece + 1) * width] = mixed.astype(out_ref.dtype)
+
+        @pl.when(rank != chunk)
+        def _():
+            for piece in range(pieces):
+                part_copy(0, chunk, piece).wait_send()
+
+
+def merge_part(front, total, pair_a, pair_b, level_weight, out_weight):
+    runs, groups = lax.axis_size("seq"), lax.axis_size("head")
+    bits = runs.bit_length() - 1
+    tokens = front.shape[0]
+    rows, width = tokens // groups, out_weight.shape[1]
+    pieces = 4
+    vmem = pl.BlockSpec(memory_space=pltpu.VMEM)
+    dma = pltpu.SemaphoreType.DMA
+    return pl.pallas_call(
+        merge_kernel,
+        in_specs=[vmem, vmem, vmem, vmem, pl.BlockSpec(memory_space=pltpu.SMEM), vmem],
+        out_specs=vmem,
+        out_shape=jax.ShapeDtypeStruct((rows, width), BF16),
+        scratch_shapes=[
+            pltpu.VMEM(front.shape, F32),
+            pltpu.VMEM(front.shape, F32),
+            pltpu.VMEM((max(bits - 1, 1),) + pair_a.shape, F32),
+            pltpu.VMEM((max(bits - 1, 1),) + pair_a.shape, F32),
+            pltpu.VMEM((bits,) + pair_a.shape, F32),
+            pltpu.VMEM((bits,) + pair_a.shape, F32),
+            pltpu.VMEM((groups, pieces, rows, width // pieces), F32),
+            pltpu.VMEM((2, groups, pieces, rows, width // pieces), F32),
+            dma((2, bits, runs // 2)),
+            dma((2, bits)),
+            dma((groups, pieces)),
+            dma((2, groups, pieces)),
+        ],
+        compiler_params=pltpu.CompilerParams(
+            collective_id=0, has_side_effects=True, vmem_limit_bytes=60 * 2**20
+        ),
+        name="merge_part",
+    )(front, total, pair_a, pair_b, level_weight, out_weight)
+
+
+def per_device(queries, key_rows, values, write_rate, decay_rate, level_weight, out_weight):
+    front, total, pair_a, pair_b = local_part(
         queries, key_rows, values, write_rate, decay_rate, level_weight
     )
-    mm = functools.partial(jnp.matmul, precision=lax.Precision.HIGHEST)
-    spans = lax.all_gather(pair[None], "seq", axis=0, tiled=True)
-    place = lax.axis_index("seq")
-    bits = lax.axis_size("seq").bit_length() - 1
-    levels = [spans]
-    for _ in range(bits - 1):
-        left, right = spans[0::2], spans[1::2]
-        out = mm(right[..., :size], left)
-        spans = out.at[..., size:].add(right[..., size:])
-        levels.append(spans)
-    weights = jnp.repeat(level_weight.astype(F32) * LEVEL_UNIT, BLOCK, axis=0)
-    front = jnp.moveaxis(front.reshape(tokens, heads, size), 1, 0)
-    added = jnp.zeros_like(front)
-    for bit in range(bits):
-        pick = jnp.maximum(jnp.right_shift(place, bit) - 1, 0)
-        span = lax.dynamic_index_in_dim(levels[bit], pick, 0, keepdims=False)
-        is_set = jnp.bitwise_and(jnp.right_shift(place, bit), 1) == 1
-        out = mm(front, span)
-        added = added + jnp.where(
-            is_set, weights[:, 1 + depth + bit][None, :, None] * out[..., size:], 0.0
-        )
-        front = jnp.where(is_set, out[..., :size], front)
-    heads_out = (total + jnp.moveaxis(added, 0, 1).reshape(tokens, heads * size)).astype(BF16)
-    mixed_out = lax.psum_scatter(
-        jnp.dot(heads_out, out_weight, preferred_element_type=F32),
-        "head",
-        scatter_dimension=0,
-        tiled=True,
-    )
-    return mixed_out.astype(BF16)
+    return merge_part(front, total, pair_a, pair_b, level_weight, out_weight)
 
 
 def solution(mesh):

time: 175 us -> 126 us (0.72)
  waiting for transfers between devices: 113 us -> 0 us
  Pallas kernels: 21.9 us -> 121 us
  matrix products: 13.5 us -> 0 us
  between operations: 13.5 us -> 0.01 us
  local copies, waits for them, and re-layouts: 9.17 us -> 4.63 us
  other arithmetic: 2.48 us -> 0 us
    pallas_call x0 -> x1, Pallas kernels: none -> 99.3 us  [merge_part(): pl.pallas_call(merge_kernel, in_specs=[vmem, vmem, vmem, vmem, pl.BlockSp...]
    reduce_scatter x1 -> x0, waiting for transfers between devices: 77.4 us -> none  [per_device(): lax.psum_scatter(jnp.dot(heads_out, out_weight, preferred_element_type=F3...]
    all_gather x1 -> x0, waiting for transfers between devices: 35.2 us -> none  [per_device(): spans = lax.all_gather(pair[None], 'seq', axis=0, tiled=True)]
    dot_general x6 -> x0, matrix products: 13.5 us -> none  [the longest x3 6.16 us: per_device(): out = mm(front, span)]
    reshape x3 -> x0, local copies, waits for them, and re-layouts: 3.19 us -> none  [the longest x1 1.56 us: per_device(): front = jnp.moveaxis(front.reshape(tokens, heads, size), 1, 0)]
    convert_element_type x1 -> x0, other arithmetic: 2.08 us -> none  [per_device(): return mixed_out.astype(BF16)]
    slice x3 -> x0, local copies, waits for them, and re-layouts: 1.96 us -> none  [the longest x2 1.95 us: per_device(): left, right = (spans[0::2], spans[1::2])]
  transfers between devices with their start and end apart: 2 -> 0, of which waited for: 2 -> 0; matrix products, arithmetic and copies ran while one was open for 1% -> 0% of each run, Pallas kernels for 0% -> 0%
where the time goes in v1:
time: 126 us
  Pallas kernels  121 us (96%)
  local copies, waits for them, and re-layouts  4.63 us (4%)
    pallas_call x1, Pallas kernels, merge_part(): pl.pallas_call(merge_kernel, in_specs=[vmem, vmem, vmem, vmem, pl.BlockSp...  99.3 us
    pallas_call x1, Pallas kernels, local_part(): pl.pallas_call(local_kernel, grid=(heads,), in_specs=[wide, wide, wide, r...  21.8 us

profile of v1, /device:TPU:15, one launch (start us, length us, event | category | flops | bytes accessed | tf_op | source)
XLA Modules:
  0.0 125.8 jit_solution(14674844029082315063)
XLA Ops:
  0.0 1.4 %reshape.6.beta_ref = f32[4,8,64]{2,1,0:T(8,128)} reshape(f32[4,512]{1,0:T(4,128)} %param.10) | data formatting | bytes 16384 | tf_op jit(solution)/shard_map/reshape | solution.py:165
  1.4 1.4 %reshape.7.decay_ref = f32[4,8,64]{2,1,0:T(8,128)} reshape(f32[4,512]{1,0:T(4,128)} %param.11) | data formatting | bytes 16384 | tf_op jit(solution)/shard_map/reshape | solution.py:166
  2.7 21.8 %local_part.1 = (f32[512,512]{1,0:T(8,128)}, f32[512,512]{1,0:T(8,128)}, f32[4,128,128]{2,1,0:T(8,128)}, f32[4,128,128]{2,1,0:T(8,128)}) custom-call(bf16[512,512]{1,0:T(8,128)(2,1)} %q_ref.1, bf16[512,512]{1,0:T(8,128)(2,1)} %k_ref.1, bf16[512,512]{1,0:T(8,128)(2,1)} %v_ref.1, f32[4,8,64]{2,1,0:T(8,128)} %reshape.6.beta_ref, f32[4,8,64]{2,1,0:T(8,128)} %reshape.7.decay_ref, ...), custom_call_target="tpu_custom_call" | custom-call | tf_op jit(solution)/shard_map/local_part/pallas_call | solution.py:149
  24.6 99.3 %merge_part.1 = bf16[128,2048]{1,0:T(8,128)(2,1)} custom-call(f32[512,512]{1,0:T(8,128)} %get-tuple-element.9.g_ref, f32[512,512]{1,0:T(8,128)} %get-tuple-element.10.o_ref, f32[4,128,128]{2,1,0:T(8,128)} %get-tuple-element.11.a_ref, f32[4,128,128]{2,1,0:T(8,128)} %get-tuple-element.12.b_ref, s32[8,7]{1,0:T(8,128)} %lw_ref.3, bf16[512,2048]{1,0:T(8,128)(2,1)} %w_ref.1), custom_call_target="tpu_custom_call" | custom-call | tf_op jit(solution)/shard_map/merge_part/pallas_call | solution.py:359
  123.9 1.9 %copy.9 = bf16[128,2048]{1,0:T(8,128)(2,1)} copy(bf16[128,2048]{1,0:T(8,128)(2,1)} %merge_part.1) | data formatting | bytes 1048576

commit v2 on v1

--- a/solution.py
+++ b/solution.py
@@ -45,8 +45,13 @@
     causal, strictly, diag = row_at >= col_at, row_at > col_at, row_at == col_at
     lower = jnp.where(causal, 1.0, 0.0).astype(F32)
     eye = jnp.where(diag, 1.0, 0.0).astype(F32)
-    beta_rows = beta_ref[0]
-    decay_rows = decay_ref[0]
+    head = pl.program_id(0)
+
+    def block_rows(ref):
+        row = ref[pl.ds(head, 1), :]
+        return jnp.concatenate([row[:, c * BLOCK : (c + 1) * BLOCK] for c in every], 0)
+
+    beta_rows, decay_rows = block_rows(beta_ref), block_rows(decay_ref)
     log_rows = -exact_dot(decay_rows, lower, NT)
     log_cols = -exact_dot(lower, decay_rows, NT)
     beta_cols = exact_dot(eye, beta_rows, NT)
@@ -142,10 +147,9 @@
     heads = write_rate.shape[0]
     tokens = queries.shape[0]
     size = queries.shape[1] // heads
-    blocks = tokens // BLOCK
     wide = pl.BlockSpec((tokens, size), lambda h: (0, h))
     state = pl.BlockSpec((1, size, size), lambda h: (h, 0, 0))
-    rates = pl.BlockSpec((1, blocks, BLOCK), lambda h: (h, 0, 0))
+    rates = pl.BlockSpec((heads, tokens), lambda h: (0, 0))
     return pl.pallas_call(
         local_kernel,
         grid=(heads,),
@@ -162,8 +166,8 @@
         queries,
         key_rows,
         values,
-        write_rate.reshape(heads, blocks, BLOCK),
-        decay_rate.reshape(heads, blocks, BLOCK),
+        write_rate,
+        decay_rate,
         level_weight,
     )
 
@@ -203,6 +207,20 @@
         barrier, runs - 1 + has_below.astype(jnp.int32) + has_above.astype(jnp.int32)
     )
 
+    def receivers(level):
+        return range(1) if level == 0 else range(1, 2**level, 2)
+
+    def relay_copy(level, what):
+        held = (got_b, got_a)[what].at[level]
+        return pltpu.make_async_remote_copy(
+            src_ref=held,
+            dst_ref=held,
+            send_sem=span_send.at[what, level, 0],
+            recv_sem=span_recv.at[what, level],
+            device_id={"seq": lax.rem(place + runs - 1, runs)},
+            device_id_type=MESH,
+        )
+
     def span_copy(level, fan, what):
         source = ((b_ref, span_b), (a_ref, span_a))[what]
         return pltpu.make_async_remote_copy(
@@ -230,21 +248,31 @@
 
         @pl.when(is_source)
         def _():
-            for fan in range(low):
+            for fan in receivers(level):
                 span_copy(level, fan, 0).start()
 
             @pl.when(later)
             def _():
-                for fan in range(low):
+                for fan in receivers(level):
                     span_copy(level, fan, 1).start()
 
         @pl.when(bit_set)
         def _():
             span_copy(level, 0, 0).wait_recv()
+            if level > 0:
+
+                @pl.when(place & 1 == 1)
+                def _():
+                    relay_copy(level, 0).start()
 
             @pl.when(later)
             def _():
                 span_copy(level, 0, 1).wait_recv()
+                if level > 0:
+
+                    @pl.when(place & 1 == 1)
+                    def _():
+                        relay_copy(level, 1).start()
 
             if level < bits - 1:
 
@@ -282,20 +310,29 @@
                 def _():
                     front[:, columns] = dot3(now, split(got_a[level, h]))
 
+        if level > 0:
+
+            @pl.when((inner >= low) & (place & 1 == 1))
+            def _():
+                relay_copy(level, 0).wait_send()
+
+                @pl.when(later)
+                def _():
+                    relay_copy(level, 1).wait_send()
+
         @pl.when(inner == low - 1)
         def _():
-            for fan in range(low):
+            for fan in receivers(level):
                 span_copy(level, fan, 0).wait_send()
 
             @pl.when(later)
             def _():
-                for fan in range(low):
+                for fan in receivers(level):
                     span_copy(level, fan, 1).wait_send()
 
-    for chunk in sorted(range(groups), key=lambda d: min(d, groups - 1 - d)):
+    def own_part(chunk, piece):
         heads_out = total[chunk * rows : (chunk + 1) * rows, :].astype(BF16)
-        for piece in range(pieces):
-            part[chunk, piece] = dot(heads_out, w_ref[:, piece * width : (piece + 1) * width])
+        return dot(heads_out, w_ref[:, piece * width : (piece + 1) * width])
 
     def part_copy(way, chunk, piece):
         return pltpu.make_async_remote_copy(
@@ -309,6 +346,7 @@
 
     def pass_on(way, chunk):
         for piece in range(pieces):
+            part[chunk, piece] = own_part(chunk, piece)
 
             @pl.when((has_below, has_above)[way])
             def _():
@@ -333,7 +371,7 @@
         @pl.when(rank == chunk)
         def _():
             for piece in range(pieces):
-                mixed = part[chunk, piece]
+                mixed = own_part(chunk, piece)
                 if chunk > 0:
                     part_copy(0, chunk, piece).wait_recv()
                     mixed = mixed + got[0, chunk, piece]

time: 126 us -> 127 us (level); the launches traced: 126 us -> 125 us
  Pallas kernels: 121 us -> 124 us
  local copies, waits for them, and re-layouts: 4.63 us -> 1.88 us
    reshape x2 -> x0, local copies, waits for them, and re-layouts: 2.75 us -> none  [the longest x1 1.37 us: local_part(): write_rate.reshape(heads, blocks, BLOCK)]
    pallas_call x1, Pallas kernels: 99.3 us -> 101 us  [merge_part(): pl.pallas_call(merge_kernel, in_specs=[vmem, vmem, vmem, vmem, pl.BlockSp...]
where the time goes in v2:
time: 127 us; the launch traced here: 125 us
  Pallas kernels  124 us (98%)
  local copies, waits for them, and re-layouts  1.88 us (1%)
    pallas_call x1, Pallas kernels, merge_part(): pl.pallas_call(merge_kernel, in_specs=[vmem, vmem, vmem, vmem, pl.BlockSp...  101 us
    pallas_call x1, Pallas kernels, local_part(): pl.pallas_call(local_kernel, grid=(heads,), in_specs=[wide, wide, wide, r...  22.4 us

profile of v2, /device:TPU:15, one launch (start us, length us, event | category | flops | bytes accessed | tf_op | source)
XLA Modules:
  0.0 125.5 jit_solution(11852977539349411827)
XLA Ops:
  0.0 22.4 %local_part.1 = (f32[512,512]{1,0:T(8,128)}, f32[512,512]{1,0:T(8,128)}, f32[4,128,128]{2,1,0:T(8,128)}, f32[4,128,128]{2,1,0:T(8,128)}) custom-call(bf16[512,512]{1,0:T(8,128)(2,1)} %q_ref.1, bf16[512,512]{1,0:T(8,128)(2,1)} %k_ref.1, bf16[512,512]{1,0:T(8,128)(2,1)} %v_ref.1, f32[4,512]{1,0:T(4,128)} %beta_ref.1, f32[4,512]{1,0:T(4,128)} %decay_ref.1, ...), custom_call_target="tpu_custom_call" | custom-call | tf_op jit(solution)/shard_map/local_part/pallas_call | solution.py:153
  22.4 101.2 %merge_part.1 = bf16[128,2048]{1,0:T(8,128)(2,1)} custom-call(f32[512,512]{1,0:T(8,128)} %get-tuple-element.9.g_ref, f32[512,512]{1,0:T(8,128)} %get-tuple-element.10.o_ref, f32[4,128,128]{2,1,0:T(8,128)} %get-tuple-element.11.a_ref, f32[4,128,128]{2,1,0:T(8,128)} %get-tuple-element.12.b_ref, s32[8,7]{1,0:T(8,128)} %lw_ref.3, bf16[512,2048]{1,0:T(8,128)(2,1)} %w_ref.1), custom_call_target="tpu_custom_call" | custom-call | tf_op jit(solution)/shard_map/merge_part/pallas_call | solution.py:397
  123.6 1.9 %copy.9 = bf16[128,2048]{1,0:T(8,128)(2,1)} copy(bf16[128,2048]{1,0:T(8,128)(2,1)} %merge_part.1) | data formatting | bytes 1048576

commit v3 on v2

--- a/solution.py
+++ b/solution.py
@@ -344,46 +344,35 @@
             device_id_type=MESH,
         )
 
-    def pass_on(way, chunk):
-        for piece in range(pieces):
-            part[chunk, piece] = own_part(chunk, piece)
-
-            @pl.when((has_below, has_above)[way])
-            def _():
-                part_copy(way, chunk, piece).wait_recv()
-                part[chunk, piece] = part[chunk, piece] + got[way, chunk, piece]
-
-            part_copy(way, chunk, piece).start()
-
-    for step in range(groups - 1):
-        up, down = groups - 1 - step, step
-
-        @pl.when(rank < up)
+    def pass_on(here, way, chunk, piece):
+        mine = own_part(chunk, piece)
+        if (here > 0, here < groups - 1)[way]:
+            part_copy(way, chunk, piece).wait_recv()
+            mine = mine + got[way, chunk, piece]
+        part[chunk, piece] = mine
+        part_copy(way, chunk, piece).start()
+
+    for here in range(groups):
+        ups = [(d, p) for d in range(groups - 1, here, -1) for p in range(pieces)]
+        downs = [(d, p) for d in range(here) for p in range(pieces)]
+        order = [(i + 1.5 * here, 0, d, p) for i, (d, p) in enumerate(ups)]
+        order += [(i + 1.5 * (groups - 1 - here), 1, d, p) for i, (d, p) in enumerate(downs)]
+
+        @pl.when(rank == here)
         def _():
-            pass_on(0, up)
-
-        @pl.when(rank > down)
-        def _():
-            pass_on(1, down)
-
-    for chunk in range(groups):
-
-        @pl.when(rank == chunk)
-        def _():
+            for _, way, chunk, piece in sorted(order):
+                pass_on(here, way, chunk, piece)
             for piece in range(pieces):
-                mixed = own_part(chunk, piece)
-                if chunk > 0:
-                    part_copy(0, chunk, piece).wait_recv()
-                    mixed = mixed + got[0, chunk, piece]
-                if chunk < groups - 1:
-                    part_copy(1, chunk, piece).wait_recv()
-                    mixed = mixed + got[1, chunk, piece]
+                mixed = own_part(here, piece)
+                if here > 0:
+                    part_copy(0, here, piece).wait_recv()
+                    mixed = mixed + got[0, here, piece]
+                if here < groups - 1:
+                    part_copy(1, here, piece).wait_recv()
+                    mixed = mixed + got[1, here, piece]
                 out_ref[:, piece * width : (piece + 1) * width] = mixed.astype(out_ref.dtype)
-
-        @pl.when(rank != chunk)
-        def _():
-            for piece in range(pieces):
-                part_copy(0, chunk, piece).wait_send()
+            for _, way, chunk, piece in order:
+                part_copy(way, chunk, piece).wait_send()
 
 
 def merge_part(front, total, pair_a, pair_b, level_weight, out_weight):

time: 127 us -> 117 us (0.921)
  Pallas kernels: 124 us -> 114 us
    pallas_call x1, Pallas kernels: 101 us -> 91.7 us  [merge_part(): pl.pallas_call(merge_kernel, in_specs=[vmem, vmem, vmem, vmem, pl.BlockSp...]
where the time goes in v3:
time: 117 us; the launch traced here: 116 us
  Pallas kernels  114 us (97%)
  local copies, waits for them, and re-layouts  1.88 us (2%)
    pallas_call x1, Pallas kernels, merge_part(): pl.pallas_call(merge_kernel, in_specs=[vmem, vmem, vmem, vmem, pl.BlockSp...  91.7 us
    pallas_call x1, Pallas kernels, local_part(): pl.pallas_call(local_kernel, grid=(heads,), in_specs=[wide, wide, wide, r...  22.4 us

profile of v3, /device:TPU:15, one launch (start us, length us, event | category | flops | bytes accessed | tf_op | source)
XLA Modules:
  0.0 115.9 jit_solution(1166773639105775076)
XLA Ops:
  0.0 22.4 %local_part.1 = (f32[512,512]{1,0:T(8,128)}, f32[512,512]{1,0:T(8,128)}, f32[4,128,128]{2,1,0:T(8,128)}, f32[4,128,128]{2,1,0:T(8,128)}) custom-call(bf16[512,512]{1,0:T(8,128)(2,1)} %q_ref.1, bf16[512,512]{1,0:T(8,128)(2,1)} %k_ref.1, bf16[512,512]{1,0:T(8,128)(2,1)} %v_ref.1, f32[4,512]{1,0:T(4,128)} %beta_ref.1, f32[4,512]{1,0:T(4,128)} %decay_ref.1, ...), custom_call_target="tpu_custom_call" | custom-call | tf_op jit(solution)/shard_map/local_part/pallas_call | solution.py:153
  22.4 91.7 %merge_part.1 = bf16[128,2048]{1,0:T(8,128)(2,1)} custom-call(f32[512,512]{1,0:T(8,128)} %get-tuple-element.9.g_ref, f32[512,512]{1,0:T(8,128)} %get-tuple-element.10.o_ref, f32[4,128,128]{2,1,0:T(8,128)} %get-tuple-element.11.a_ref, f32[4,128,128]{2,1,0:T(8,128)} %get-tuple-element.12.b_ref, s32[8,7]{1,0:T(8,128)} %lw_ref.3, bf16[512,2048]{1,0:T(8,128)(2,1)} %w_ref.1), custom_call_target="tpu_custom_call" | custom-call | tf_op jit(solution)/shard_map/merge_part/pallas_call | solution.py:386
  114.0 1.9 %copy.9 = bf16[128,2048]{1,0:T(8,128)(2,1)} copy(bf16[128,2048]{1,0:T(8,128)(2,1)} %merge_part.1) | data formatting | bytes 1048576
